TPU v7x, 32 devices: a whole 2x2x4 slice. The times are simulated.
32 devices in a mesh: sect: 4 (over x, core), batch: 8 (over z, y).
Axes of the slice: x: 2, y: 2, z: 4, core: 2. Of those that a mesh axis runs over, the one named last changes fastest.
Arguments:
- warm: bfloat16 [8192, 640], P(('sect', 'batch')), may hold values from -6 to 6
- latents: float32 [4, 1024], P(None, 'batch'), may hold values from -6 to 6
- timesteps: int32 [5], replicated, may hold values from 300 to 599
- assign: int32 [8], P('batch'), may hold values from 0 to 7, each once
- prompts: bfloat16 [8, 640], P('batch'), may hold values from -6 to 6
- w_in: bfloat16 [2560, 2560], P('sect'), may hold values from -0.25 to 0.25
- time_w: bfloat16 [2560, 640], P('sect'), may hold values from -0.25 to 0.25
- w_out: bfloat16 [5120, 640], P(('sect', 'batch')), may hold values from -0.15625 to 0.15625
- conv_in_w: bfloat16 [4, 640], replicated, may hold values from -3 to 3
- conv_out_w: bfloat16 [4, 640], replicated, may hold values from -0.25 to 0.25
Outputs:
- segments: bfloat16 [8192, 640], P(('sect', 'batch'))
- final_latents: float32 [4, 1024], P('sect', 'batch')
Inputs may be any that keep to these rules, and one draw needn't show every extreme that they name: `assign`: each prompt is assigned to exactly one prompt batch.
All inputs are finite; a program needn't handle non-finite values.
Results may differ from a plain program's by a relative error of at most 0.015.
Values may be sent and summed in bfloat16 or wider, within the bound.
A program may use at most 64 MiB of HBM per device.

v0:
```python
import math

import jax
import jax.numpy as jnp
from jax import lax
from jax.sharding import PartitionSpec as P

guidance_scale = 3.0


def passed_along(shard, axis, by):
    devices = lax.axis_size(axis)
    pairs = [(i, i + by) for i in range(devices) if 0 <= i + by < devices]
    return lax.ppermute(shard, axis, pairs)


def from_behind(block, axis, distance):
    devices = range(lax.axis_size(axis))
    route = [((i - distance) % len(devices), i) for i in devices]
    return lax.ppermute(block, axis, route)


def broadcast(block, axis, source):
    block = jnp.where(lax.axis_index(axis) == source, block, jnp.zeros_like(block))
    return lax.psum(block, axis)


def sinusoid(time_value, channels):
    half_width = channels // 2
    frequency = jnp.exp(-math.log(10000.0) * jnp.arange(half_width, dtype=jnp.float32) / half_width)
    angles = time_value.astype(jnp.float32) * frequency
    return jnp.concatenate([jnp.cos(angles), jnp.sin(angles)])


def alpha_bar(time_value):
    phase_angle = (time_value.astype(jnp.float32) / 1000.0 + 0.008) / 1.008 * (math.pi / 2)
    return jnp.cos(phase_angle) ** 2


def rms_norm(values):
    return values * lax.rsqrt(jnp.mean(values * values, axis=-1, keepdims=True) + 1e-06)


def feed_block(inputs, time_vec, cond_rows, weight_in, weight_out, hidden_units):
    summed = inputs + time_vec + cond_rows
    normed = rms_norm(summed).astype(jnp.bfloat16)
    projected = jnp.dot(normed, weight_in, preferred_element_type=jnp.float32)
    hidden = (
        projected[:, :hidden_units] * jax.nn.gelu(projected[:, hidden_units:], approximate=False)
    ).astype(jnp.bfloat16)
    return (summed + jnp.dot(hidden, weight_out, preferred_element_type=jnp.float32)).astype(
        jnp.bfloat16
    )


def on_device(
    warm, latents, timesteps, assign, prompts, w_in, time_w, w_out, conv_in_w, conv_out_w
):
    section = lax.axis_index("sect")
    sect_count = lax.axis_size("sect")
    last_index = sect_count - 1
    w_out_all, table = (
        lax.all_gather(w_out, "batch", axis=0, tiled=True),
        lax.all_gather(prompts, "batch", axis=0, tiled=True),
    )
    positions = latents.shape[1]
    channels = warm.shape[1]
    hidden_units = w_out_all.shape[0]
    picker = (jnp.arange(table.shape[0], dtype=jnp.int32)[None, :] == assign[:, None]).astype(
        jnp.bfloat16
    )
    chosen = jnp.dot(picker, table, preferred_element_type=jnp.float32)
    cond = jnp.concatenate(
        [
            jnp.broadcast_to(chosen, (positions, channels)),
            jnp.zeros((positions, channels), jnp.float32),
        ],
        axis=0,
    )
    segment = warm
    latent = latents
    for step_index in range(timesteps.shape[0] - 1):
        time_now = timesteps[step_index]
        time_next = timesteps[step_index + 1]
        received = passed_along(segment, "sect", 1)
        skipped = from_behind(segment, "sect", -1)
        embedded = jax.nn.silu(sinusoid(time_now, channels)).astype(jnp.bfloat16)
        first = lax.dot_general(
            latent.astype(jnp.bfloat16),
            conv_in_w,
            (((0,), (0,)), ((), ())),
            preferred_element_type=jnp.float32,
        ).astype(jnp.bfloat16)
        first = jnp.concatenate([first, first], axis=0)
        inputs = jnp.where(section == 0, first, received).astype(jnp.float32)
        inputs = (inputs + skipped.astype(jnp.float32)) * 0.5
        time_vec = jnp.dot(embedded[None, :], time_w, preferred_element_type=jnp.float32)
        segment = feed_block(inputs, time_vec, cond, w_in, w_out_all, hidden_units)
        activated = jax.nn.silu(rms_norm(segment.astype(jnp.float32))).astype(jnp.bfloat16)
        noise = lax.dot_general(
            conv_out_w, activated, (((1,), (1,)), ((), ())), preferred_element_type=jnp.float32
        )
        guided = noise[:, positions:] + guidance_scale * (
            noise[:, :positions] - noise[:, positions:]
        )
        bar_now = alpha_bar(time_now)
        bar_next = alpha_bar(time_next)
        clean = (latent - jnp.sqrt(1.0 - bar_now) * guided) / jnp.sqrt(bar_now)
        updated = jnp.sqrt(bar_next) * clean + jnp.sqrt(1.0 - bar_next) * guided
        latent = broadcast(updated, "sect", last_index)
    channels_here = latent.shape[0] // sect_count
    own_latent = lax.dynamic_slice_in_dim(latent, section * channels_here, channels_here, 0)
    return (segment, own_latent)


def solution(mesh):
    return jax.shard_map(
        on_device,
        mesh=mesh,
        in_specs=(
            P(("sect", "batch"), None),
            P(None, "batch"),
            P(),
            P("batch"),
            P("batch", None),
            P("sect", None),
            P("sect", None),
            P(("sect", "batch"), None),
            P(),
            P(),
        ),
        out_specs=(P(("sect", "batch"), None), P("sect", "batch")),
        check_vma=False,
    )
```

profile of v0, /device:TPU:0, one launch (start us, length us, event | category | flops | bytes accessed | tf_op | source)
XLA Modules:
  0.0 147.3 jit_solution(3572738905589902597)
XLA Ops:
  7.2 0.7 all-gather.3.cloned.1.call-update
  7.9 3.2 %collective-permute-start = (bf16[256,640]{1,0:T(8,128)(2,1)}, bf16[256,640]{1,0:T(8,128)(2,1)}, u32[]{:S(2)}, u32[]{:S(2)}) collective-permute-start(bf16[256,640]{1,0:T(8,128)(2,1)} %param.10), channel_id=1, source_target_pairs={{0,8},{8,16},{16,24},{1,9},{9,17},{17,25},{2,10},{10,18},{18,26},{... | collective-permute-start | bytes 983048 | tf_op jit(solution)/shard_map/ppermute | solution.py:14
  11.1 0.6 collective-permute-start.1
  11.8 1.5 %fusion.362 = (s32[1]{0:T(128)}, s32[1]{0:T(128)}, s32[1]{0:T(128)}, s32[1]{0:T(128)}, s32[1]{0:T(128)}) fusion(s32[5]{0:T(128)} %param.12), kind=kLoop, calls=%fused_computation.457 | loop fusion | bytes 40 | tf_op jit(solution)/shard_map/slice | solution.py:84
  18.7 31.3 %all-gather = bf16[8,1,640]{2,1,0:T(2,128)(2,1)S(1)} all-gather(bf16[1,1,640]{2,1,0:T(2,128)(2,1)} %bitcast.47), channel_id=1, replica_groups=mesh['sect'=4,'batch'=8] {'batch'}, dimensions={0}, use_global_device_ids=true | all-gather | bytes 11520 | tf_op jit(solution)/shard_map/all_gather | solution.py:64
  50.0 1.4 convolution_reduce_fusion.4
  51.4 1.4 convolution_reduce_fusion.3
  53.8 1.4 multiply_reduce_fusion.3
  55.2 3.8 %fusion.196 = f32[256,2560]{1,0:T(8,128)} fusion(bf16[640,2560]{1,0:T(8,128)(2,1)S(1)} %copy-done, f32[256]{0:T(256)S(1)} %add_rsqrt_fusion.7, f32[128,640]{1,0:T(8,128)S(1)} %broadcast_in_dim.2, bf16[256,640]{1,0:T(8,128)(2,1)} %collective-permute-done.1, bf16[256,640]{1,0:T(8,128)(2,1)} %collective-permute-done, ...), kind=kOutput, calls=%fused_computation.265 | convolution fusion | flops 840990720 | bytes 7048705 | tf_op jit(solution)/shard_map/dot_general | solution.py:47
  59.0 6.4 %fusion.72 = (f32[256]{0:T(256)S(1)}, bf16[256,640]{1,0:T(8,128)(2,1)}) fusion(bf16[1280,640]{1,0:T(8,128)(2,1)} %all-gather.3.cloned.1.call-done, f32[256,2560]{1,0:T(8,128)} %fusion.196, f32[128,640]{1,0:T(8,128)} %copy-done.1, f32[640]{0:T(1024)S(1)} %convolution_reduce_fusion.4, bf16[256,640]{1,0:T(8,128)(2,1)} %collective-permute-done.1, ...), kind=kOutput, calls=%fused_computation.137 | convolution fusion | flops 443678464 | bytes 5737985 | tf_op jit(solution)/shard_map/dot_general | solution.py:51
  65.4 2.0 %collective-permute-start.2 = (bf16[256,640]{1,0:T(8,128)(2,1)}, bf16[256,640]{1,0:T(8,128)(2,1)}, u32[]{:S(2)}, u32[]{:S(2)}) collective-permute-start(bf16[256,640]{1,0:T(8,128)(2,1)} %get-tuple-element.8), channel_id=1, source_target_pairs={{0,8},{8,16},{16,24},{1,9},{9,17},{17,25},{2,10},{10,18},{18,26},{... | collective-permute-start | bytes 983048 | tf_op jit(solution)/shard_map/ppermute | solution.py:14
  67.4 1.3 convolution_bitcast_fusion.3
  68.8 9.1 %psum.28 = f32[4,128]{1,0:T(4,128)S(1)} all-reduce(f32[4,128]{1,0:T(4,128)S(1)} %add_select_fusion.3), channel_id=1, replica_groups=mesh['sect'=4,'batch'=8] {'sect'}, use_global_device_ids=true, to_apply=%region_2.3 | all-reduce | flops 512 | bytes 4096 | tf_op jit(solution)/shard_map/psum | solution.py:25
  78.2 1.4 multiply_reduce_fusion.2
  79.6 2.4 %fusion.197 = f32[256,2560]{1,0:T(8,128)S(1)} fusion(bf16[640,2560]{1,0:T(8,128)(2,1)S(1)} %copy-done, f32[256]{0:T(256)S(1)} %add_rsqrt_fusion.5, f32[128,640]{1,0:T(8,128)S(1)} %copy-done.2, bf16[256,640]{1,0:T(8,128)(2,1)} %collective-permute-done.3, bf16[256,640]{1,0:T(8,128)(2,1)} %collective-permute-done.2, ...), kind=kOutput, calls=%fused_computation.266 | convolution fusion | flops 840990720 | bytes 7048705 | tf_op jit(solution)/shard_map/dot_general | solution.py:47
  82.0 5.2 %fusion.73 = (f32[256]{0:T(256)S(1)}, bf16[256,640]{1,0:T(8,128)(2,1)}) fusion(bf16[1280,640]{1,0:T(8,128)(2,1)S(1)} %copy-done.8, f32[256,2560]{1,0:T(8,128)S(1)} %fusion.197, f32[128,640]{1,0:T(8,128)S(1)} %copy-done.2, f32[640]{0:T(1024)S(1)} %convolution_reduce_fusion.3, bf16[256,640]{1,0:T(8,128)(2,1)} %collective-permute-done.3, ...), kind=kOutput, calls=%fused_computation.138 | convolution fusion | flops 443678464 | bytes 5737985 | tf_op jit(solution)/shard_map/dot_general | solution.py:51
  87.2 3.0 %collective-permute-start.4 = (bf16[256,640]{1,0:T(8,128)(2,1)}, bf16[256,640]{1,0:T(8,128)(2,1)}, u32[]{:S(2)}, u32[]{:S(2)}) collective-permute-start(bf16[256,640]{1,0:T(8,128)(2,1)} %get-tuple-element.10), channel_id=1, source_target_pairs={{0,8},{8,16},{16,24},{1,9},{9,17},{17,25},{2,10},{10,18},{18,26},{... | collective-permute-start | bytes 983048 | tf_op jit(solution)/shard_map/ppermute | solution.py:14
  90.2 1.3 convolution_bitcast_fusion.2
  91.6 9.8 %psum.29 = f32[4,128]{1,0:T(4,128)S(1)} all-reduce(f32[4,128]{1,0:T(4,128)S(1)} %add_select_fusion.2), channel_id=1, replica_groups=mesh['sect'=4,'batch'=8] {'sect'}, use_global_device_ids=true, to_apply=%region_5.6 | all-reduce | flops 512 | bytes 4096 | tf_op jit(solution)/shard_map/psum | solution.py:25
  101.6 1.4 multiply_reduce_fusion.1
  103.0 2.4 %fusion.198 = f32[256,2560]{1,0:T(8,128)S(1)} fusion(bf16[640,2560]{1,0:T(8,128)(2,1)S(1)} %copy-done, f32[256]{0:T(256)S(1)} %add_rsqrt_fusion.3, f32[128,640]{1,0:T(8,128)S(1)} %copy-done.3, bf16[256,640]{1,0:T(8,128)(2,1)} %collective-permute-done.5, bf16[256,640]{1,0:T(8,128)(2,1)} %collective-permute-done.4, ...), kind=kOutput, calls=%fused_computation.267 | convolution fusion | flops 840990720 | bytes 7048705 | tf_op jit(solution)/shard_map/dot_general | solution.py:47
  105.4 5.2 %fusion.74 = (f32[256]{0:T(256)S(1)}, bf16[256,640]{1,0:T(8,128)(2,1)}) fusion(bf16[1280,640]{1,0:T(8,128)(2,1)S(1)} %copy-done.9, f32[256,2560]{1,0:T(8,128)S(1)} %fusion.198, f32[128,640]{1,0:T(8,128)S(1)} %copy-done.3, f32[640]{0:T(1024)S(1)} %convolution_reduce_fusion.2, bf16[256,640]{1,0:T(8,128)(2,1)} %collective-permute-done.5, ...), kind=kOutput, calls=%fused_computation.139 | convolution fusion | flops 443678464 | bytes 5737985 | tf_op jit(solution)/shard_map/dot_general | solution.py:51
  110.6 2.0 %collective-permute-start.6 = (bf16[256,640]{1,0:T(8,128)(2,1)}, bf16[256,640]{1,0:T(8,128)(2,1)}, u32[]{:S(2)}, u32[]{:S(2)}) collective-permute-start(bf16[256,640]{1,0:T(8,128)(2,1)} %get-tuple-element.12), channel_id=1, source_target_pairs={{0,8},{8,16},{16,24},{1,9},{9,17},{17,25},{2,10},{10,18},{18,26},{... | collective-permute-start | bytes 983048 | tf_op jit(solution)/shard_map/ppermute | solution.py:14
  112.8 1.3 convolution_bitcast_fusion.1
  114.2 10.5 %psum.30 = f32[4,128]{1,0:T(4,128)S(1)} all-reduce(f32[4,128]{1,0:T(4,128)S(1)} %add_select_fusion.1), channel_id=1, replica_groups=mesh['sect'=4,'batch'=8] {'sect'}, use_global_device_ids=true, to_apply=%region_8.9 | all-reduce | flops 512 | bytes 4096 | tf_op jit(solution)/shard_map/psum | solution.py:25
  125.0 1.4 multiply_reduce_fusion
  126.4 2.4 %fusion.199 = f32[256,2560]{1,0:T(8,128)S(1)} fusion(bf16[640,2560]{1,0:T(8,128)(2,1)S(1)} %copy-done, f32[256]{0:T(256)S(1)} %add_rsqrt_fusion.1, f32[128,640]{1,0:T(8,128)S(1)} %copy-done.4, bf16[256,640]{1,0:T(8,128)(2,1)} %collective-permute-done.7, bf16[256,640]{1,0:T(8,128)(2,1)} %collective-permute-done.6, ...), kind=kOutput, calls=%fused_computation.268 | convolution fusion | flops 840990720 | bytes 7048705 | tf_op jit(solution)/shard_map/dot_general | solution.py:47
  128.8 4.6 %fusion.75 = (f32[256]{0:T(256)S(1)}, bf16[256,640]{1,0:T(8,128)(2,1)S(1)}) fusion(bf16[1280,640]{1,0:T(8,128)(2,1)S(1)} %copy-done.10, f32[256,2560]{1,0:T(8,128)S(1)} %fusion.199, f32[128,640]{1,0:T(8,128)S(1)} %copy-done.4, f32[640]{0:T(1024)S(1)} %convolution_reduce_fusion.1, bf16[256,640]{1,0:T(8,128)(2,1)} %collective-permute-done.7, ...), kind=kOutput, calls=%fused_computation.140 | convolution fusion | flops 443678464 | bytes 5737985 | tf_op jit(solution)/shard_map/dot_general | solution.py:51
  133.4 0.3 convolution_bitcast_fusion
  133.8 0.4 copy-done.12
  134.2 5.8 %psum.31 = f32[4,128]{1,0:T(4,128)S(1)} all-reduce(f32[4,128]{1,0:T(4,128)S(1)} %add_select_fusion), channel_id=1, replica_groups=mesh['sect'=4,'batch'=8] {'sect'}, use_global_device_ids=true, to_apply=%region_11.12 | all-reduce | flops 512 | bytes 4096 | tf_op jit(solution)/shard_map/psum | solution.py:25
  139.9 0.5 constant_dynamic-slice_fusion
  (70 shorter events, 2.8 us)
Async XLA Ops:
  7.2 48.0 %copy-start = (bf16[640,2560]{1,0:T(8,128)(2,1)S(1)}, bf16[640,2560]{1,0:T(8,128)(2,1)}, u32[]{:S(2)}) copy-start(bf16[640,2560]{1,0:T(8,128)(2,1)} %param.15) | copy-start | bytes 9830404
  7.2 51.8 %all-gather.3.cloned.1.call-start = ((), (), s32[]{:S(2)}) async-start(), calls=%async_computation | async-start | bytes 1843200 | tf_op jit(solution)/shard_map/all_gather | solution.py:63
  7.9 45.8 %collective-permute-start = (bf16[256,640]{1,0:T(8,128)(2,1)}, bf16[256,640]{1,0:T(8,128)(2,1)}, u32[]{:S(2)}, u32[]{:S(2)}) collective-permute-start(bf16[256,640]{1,0:T(8,128)(2,1)} %param.10), channel_id=1, source_target_pairs={{0,8},{8,16},{16,24},{1,9},{9,17},{17,25},{2,10},{10,18},{18,26},{... | collective-permute-start | bytes 983048 | tf_op jit(solution)/shard_map/ppermute | solution.py:14
  11.1 42.6 %collective-permute-start.1 = (bf16[256,640]{1,0:T(8,128)(2,1)}, bf16[256,640]{1,0:T(8,128)(2,1)}, u32[]{:S(2)}, u32[]{:S(2)}) collective-permute-start(bf16[256,640]{1,0:T(8,128)(2,1)} %param.10), channel_id=1, source_target_pairs={{8,0},{16,8},{24,16},{0,24},{9,1},{17,9},{25,17},{1,25},{10,2},{18... | collective-permute-start | bytes 983048 | tf_op jit(solution)/shard_map/ppermute | solution.py:20
  18.7 34.1 %copy-start.5 = (bf16[640,640]{1,0:T(8,128)(2,1)S(1)}, bf16[640,640]{1,0:T(8,128)(2,1)}, u32[]{:S(2)}) copy-start(bf16[640,640]{1,0:T(8,128)(2,1)} %param.16) | copy-start | bytes 2457604
  51.4 2.1 %copy-start.6 = (bf16[4,640]{1,0:T(4,128)(2,1)S(1)}, bf16[4,640]{1,0:T(4,128)(2,1)}, u32[]{:S(2)}) copy-start(bf16[4,640]{1,0:T(4,128)(2,1)} %param.18) | copy-start | bytes 15364
  51.4 2.1 %copy-start.7 = (f32[4,128]{1,0:T(4,128)S(1)}, f32[4,128]{1,0:T(4,128)}, u32[]{:S(2)}) copy-start(f32[4,128]{1,0:T(4,128)} %param.11) | copy-start | bytes 6148
  53.8 1.4 copy-start.1
  59.0 8.4 %copy-start.11 = (bf16[4,640]{1,0:T(4,128)(2,1)S(1)}, bf16[4,640]{1,0:T(4,128)(2,1)}, u32[]{:S(2)}) copy-start(bf16[4,640]{1,0:T(4,128)(2,1)} %param.19) | copy-start | bytes 15364
  65.4 12.8 %collective-permute-start.2 = (bf16[256,640]{1,0:T(8,128)(2,1)}, bf16[256,640]{1,0:T(8,128)(2,1)}, u32[]{:S(2)}, u32[]{:S(2)}) collective-permute-start(bf16[256,640]{1,0:T(8,128)(2,1)} %get-tuple-element.8), channel_id=1, source_target_pairs={{0,8},{8,16},{16,24},{1,9},{9,17},{17,25},{2,10},{10,18},{18,26},{... | collective-permute-start | bytes 983048 | tf_op jit(solution)/shard_map/ppermute | solution.py:14
  67.4 10.8 %collective-permute-start.3 = (bf16[256,640]{1,0:T(8,128)(2,1)}, bf16[256,640]{1,0:T(8,128)(2,1)}, u32[]{:S(2)}, u32[]{:S(2)}) collective-permute-start(bf16[256,640]{1,0:T(8,128)(2,1)} %get-tuple-element.8), channel_id=1, source_target_pairs={{8,0},{16,8},{24,16},{0,24},{9,1},{17,9},{25,17},{1,25},{10,2},{18... | collective-permute-start | bytes 983048 | tf_op jit(solution)/shard_map/ppermute | solution.py:20
  78.0 1.6 %copy-start.2 = (f32[128,640]{1,0:T(8,128)S(1)}, f32[128,640]{1,0:T(8,128)}, u32[]{:S(2)}) copy-start(f32[128,640]{1,0:T(8,128)} %copy-done.1) | copy-start | bytes 983044
  79.6 2.4 %copy-start.8 = (bf16[1280,640]{1,0:T(8,128)(2,1)S(1)}, bf16[1280,640]{1,0:T(8,128)(2,1)}, u32[]{:S(2)}) copy-start(bf16[1280,640]{1,0:T(8,128)(2,1)} %all-gather.3.cloned.1.call-done) | copy-start | bytes 4915204
  87.2 14.4 %collective-permute-start.4 = (bf16[256,640]{1,0:T(8,128)(2,1)}, bf16[256,640]{1,0:T(8,128)(2,1)}, u32[]{:S(2)}, u32[]{:S(2)}) collective-permute-start(bf16[256,640]{1,0:T(8,128)(2,1)} %get-tuple-element.10), channel_id=1, source_target_pairs={{0,8},{8,16},{16,24},{1,9},{9,17},{17,25},{2,10},{10,18},{18,26},{... | collective-permute-start | bytes 983048 | tf_op jit(solution)/shard_map/ppermute | solution.py:14
  90.2 11.5 %collective-permute-start.5 = (bf16[256,640]{1,0:T(8,128)(2,1)}, bf16[256,640]{1,0:T(8,128)(2,1)}, u32[]{:S(2)}, u32[]{:S(2)}) collective-permute-start(bf16[256,640]{1,0:T(8,128)(2,1)} %get-tuple-element.10), channel_id=1, source_target_pairs={{8,0},{16,8},{24,16},{0,24},{9,1},{17,9},{25,17},{1,25},{10,2},{18... | collective-permute-start | bytes 983048 | tf_op jit(solution)/shard_map/ppermute | solution.py:20
  101.4 1.6 %copy-start.3 = (f32[128,640]{1,0:T(8,128)S(1)}, f32[128,640]{1,0:T(8,128)}, u32[]{:S(2)}) copy-start(f32[128,640]{1,0:T(8,128)} %copy-done.1) | copy-start | bytes 983044
  103.0 2.4 %copy-start.9 = (bf16[1280,640]{1,0:T(8,128)(2,1)S(1)}, bf16[1280,640]{1,0:T(8,128)(2,1)}, u32[]{:S(2)}) copy-start(bf16[1280,640]{1,0:T(8,128)(2,1)} %all-gather.3.cloned.1.call-done) | copy-start | bytes 4915204
  110.6 14.4 %collective-permute-start.6 = (bf16[256,640]{1,0:T(8,128)(2,1)}, bf16[256,640]{1,0:T(8,128)(2,1)}, u32[]{:S(2)}, u32[]{:S(2)}) collective-permute-start(bf16[256,640]{1,0:T(8,128)(2,1)} %get-tuple-element.12), channel_id=1, source_target_pairs={{0,8},{8,16},{16,24},{1,9},{9,17},{17,25},{2,10},{10,18},{18,26},{... | collective-permute-start | bytes 983048 | tf_op jit(solution)/shard_map/ppermute | solution.py:14
  112.6 12.4 %collective-permute-start.7 = (bf16[256,640]{1,0:T(8,128)(2,1)}, bf16[256,640]{1,0:T(8,128)(2,1)}, u32[]{:S(2)}, u32[]{:S(2)}) collective-permute-start(bf16[256,640]{1,0:T(8,128)(2,1)} %get-tuple-element.12), channel_id=1, source_target_pairs={{8,0},{16,8},{24,16},{0,24},{9,1},{17,9},{25,17},{1,25},{10,2},{18... | collective-permute-start | bytes 983048 | tf_op jit(solution)/shard_map/ppermute | solution.py:20
  124.7 1.6 %copy-start.4 = (f32[128,640]{1,0:T(8,128)S(1)}, f32[128,640]{1,0:T(8,128)}, u32[]{:S(2)}) copy-start(f32[128,640]{1,0:T(8,128)} %copy-done.1) | copy-start | bytes 983044
  126.4 2.4 %copy-start.10 = (bf16[1280,640]{1,0:T(8,128)(2,1)S(1)}, bf16[1280,640]{1,0:T(8,128)(2,1)}, u32[]{:S(2)}) copy-start(bf16[1280,640]{1,0:T(8,128)(2,1)} %all-gather.3.cloned.1.call-done) | copy-start | bytes 4915204
  133.4 0.7 copy-start.12
Sparse Core Ops, SparseCore 0:
  10.2 47.5 all-gather.2
where the time goes:
time: 148 us; the launch traced here: 147 us
  blocking collectives  66.5 us (45%)
  matrix products  41 us (28%)
  between operations  19.2 us (13%)
  starting transfers between devices  11.1 us (8%)
  other arithmetic  6.24 us (4%)
  local copies, waits for them, and re-layouts  2.51 us (2%)
    psum x4, blocking collectives, broadcast(): return lax.psum(block, axis)  35.2 us
    all_gather x1, blocking collectives, on_device(): lax.all_gather(prompts, 'batch', axis=0, tiled=True)  31.3 us
    dot_general x4, matrix products, feed_block(): jnp.dot(hidden, weight_out, preferred_element_type=jnp.float32)  21.4 us
    dot_general x4, matrix products, feed_block(): projected = jnp.dot(normed, weight_in, preferred_element_type=jnp.float32)  11 us
    ppermute x4, starting transfers between devices, passed_along(): return lax.ppermute(shard, axis, pairs)  10.2 us
    reduce_sum x4, other arithmetic, rms_norm(): jnp.mean(values * values, axis=-1, keepdims=True) + 1e-06  5.44 us
    dot_general x4, matrix products, on_device(): lax.dot_general(conv_out_w, activated, (((1,), (1,)), ((), ())), preferre...  4.33 us
    dot_general x4, matrix products, on_device(): jnp.dot(embedded[None, :], time_w, preferred_element_type=jnp.float32)  3.26 us
  transfers between devices with their start and end apart: 9, of which 0 were waited for; matrix products, arithmetic and copies ran while one was open for 11% of the time, Pallas kernels for 0%

commit v1 on v0

v1 whole, which is shorter than its diff:
```python
import functools
import math

import jax
import jax.numpy as jnp
from jax import lax
from jax.experimental import pallas as pl
from jax.experimental.pallas import tpu as pltpu
from jax.sharding import PartitionSpec as P

guidance_scale = 3.0
MESH = pl.DeviceIdType.MESH
F32 = jnp.float32
BF16 = jnp.bfloat16
CHUNKS = 2


def kernel(
    sects, batches, gathered,
    ts_ref, assign_ref, warm_ref, lat_ref, prompts_ref, w_in_ref, time_w_ref, w_out_ref, cin_ref, cout_ref,
    oseg_ref, olat_ref,
    w_in, time_w, w_all, xbuf, kbuf, ybuf, a_scr, h_scr, tv, roots, rests, cond, ptab, pown,
    cin, cout, lat, latin, latout, fin, fin_in,
    load_sem, x_send, x_recv, k_send, k_recv, l_send, l_recv, f_send, f_recv,
    p_send, p_recv, g_line, g_side, g_recv,
):
    s = lax.axis_index("sect")
    me = lax.axis_index("batch")
    steps = ts_ref.shape[0] - 1
    _, positions, channels = warm_ref.shape
    hidden = w_all.shape[0]
    part = positions // CHUNKS
    up = lax.rem(s + 1, sects)
    down = lax.rem(s + sects - 1, sects)
    last = sects - 1

    loads = [
        pltpu.make_async_copy(time_w_ref, time_w, load_sem.at[0]),
        pltpu.make_async_copy(w_in_ref, w_in, load_sem.at[1]),
    ]
    if gathered:
        loads.append(pltpu.make_async_copy(w_out_ref, w_all, load_sem.at[2]))
    else:
        depth = w_out_ref.shape[0]
        own_rows = pl.ds(pl.multiple_of(me * depth, depth), depth)
        loads.append(pltpu.make_async_copy(w_out_ref, w_all.at[own_rows], load_sem.at[2]))
    for copy in loads:
        copy.start()

    barrier = pltpu.get_barrier_semaphore()
    for d in range(1, sects):
        pl.semaphore_signal(barrier, inc=1, device_id={"sect": lax.rem(s + d, sects)}, device_id_type=MESH)
    met = sects - 1
    if not gathered:
        for d in range(1, batches):
            pl.semaphore_signal(barrier, inc=1, device_id={"batch": lax.rem(me + d, batches)}, device_id_type=MESH)
        met += batches - 1
        pown[...] = prompts_ref[...].astype(F32)
    pl.semaphore_wait(barrier, met)

    def rows(c):
        return pl.ds(c * part, part)

    def x_copy(src, slot, c):
        return pltpu.make_async_remote_copy(
            src_ref=src, dst_ref=xbuf.at[slot, :, rows(c), :], send_sem=x_send.at[slot, c],
            recv_sem=x_recv.at[slot, c], device_id={"sect": up}, device_id_type=MESH)

    def k_copy(src, slot, c):
        return pltpu.make_async_remote_copy(
            src_ref=src, dst_ref=kbuf.at[slot, :, rows(c), :], send_sem=k_send.at[slot, c],
            recv_sem=k_recv.at[slot, c], device_id={"sect": down}, device_id_type=MESH)

    def l_copy(slot, c):
        return pltpu.make_async_remote_copy(
            src_ref=latout.at[slot, rows(c), :], dst_ref=latin.at[slot, rows(c), :], send_sem=l_send.at[slot, c],
            recv_sem=l_recv.at[slot, c], device_id={"sect": 0}, device_id_type=MESH)

    def f_copy(d):
        return pltpu.make_async_remote_copy(
            src_ref=fin.at[d], dst_ref=fin_in, send_sem=f_send.at[d],
            recv_sem=f_recv, device_id={"sect": d}, device_id_type=MESH)

    if not gathered:
        z, y = me // 2, lax.rem(me, 2)
        length = batches // 2
        side = z * 2 + (1 - y)

        def p_copy(d):
            return pltpu.make_async_remote_copy(
                src_ref=pown, dst_ref=ptab.at[me], send_sem=p_send.at[d], recv_sem=p_recv.at[me],
                device_id={"batch": lax.rem(me + d, batches)}, device_id_type=MESH)

        def block(b):
            return w_all.at[pl.ds(pl.multiple_of(b * depth, depth), depth)]

        def g_copy(b, to, sems, src=None):
            return pltpu.make_async_remote_copy(
                src_ref=block(b) if src is None else src, dst_ref=block(b), send_sem=sems.at[b],
                recv_sem=g_recv.at[b], device_id={"batch": to}, device_id_type=MESH)

        def g_arrived(b):
            pltpu.make_async_copy(block(b), block(b), g_recv.at[b]).wait()

        for d in range(1, batches):
            p_copy(d).start()

        @pl.when(z < length - 1)
        def _():
            g_copy(me, me + 2, g_line.at[0], w_out_ref).start()

        @pl.when(z > 0)
        def _():
            g_copy(me, me - 2, g_line.at[1], w_out_ref).start()

        g_copy(me, side, g_side, w_out_ref).start()

    for c in range(CHUNKS):
        @pl.when(s < last)
        def _(c=c):
            x_copy(warm_ref.at[:, rows(c), :], 0, c).start()
        k_copy(warm_ref.at[:, rows(c), :], 0, c).start()

    cin[...] = jnp.zeros_like(cin)
    cout[...] = jnp.zeros_like(cout)
    levels = cin_ref.shape[0]
    cin[0:levels, :] = cin_ref[...].astype(F32)
    cout[0:levels, :] = cout_ref[...].astype(F32)
    lat[...] = jnp.zeros_like(lat)
    lat[0:levels, :] = lat_ref[...]
    turned = lat[...].T
    lat[...] = turned
    latin[0] = turned.astype(BF16)
    which = lax.broadcasted_iota(jnp.int32, (16, 128), 0)
    times = jnp.zeros((16, 128), F32)
    for i in range(steps + 1):
        times = jnp.where(which == i, ts_ref[i].astype(F32), times)
    bar = jnp.cos((times / 1000.0 + 0.008) / 1.008 * (math.pi / 2)) ** 2
    roots[...] = jnp.sqrt(bar)
    rests[...] = jnp.sqrt(1.0 - bar)
    half = channels // 2
    lane = lax.broadcasted_iota(jnp.int32, (16, channels), 1)
    wave = jnp.where(lane < half, lane, lane - half).astype(F32)
    frequency = jnp.exp(-math.log(10000.0) * wave / half)
    angles = jnp.concatenate([times] * (channels // 128), axis=1) * frequency
    waves = jnp.where(lane < half, jnp.cos(angles), jnp.sin(angles))
    embedded = (waves * (1.0 / (1.0 + jnp.exp(-waves)))).astype(BF16)
    loads[0].wait()
    tv[...] = jnp.dot(embedded, time_w[...], preferred_element_type=F32)

    if gathered:
        cond[...] = prompts_ref[...]
    else:
        ptab[me] = pown[...]
        for d in range(1, batches):
            b = lax.rem(me + d, batches)
            pltpu.make_async_copy(ptab.at[b], ptab.at[b], p_recv.at[b]).wait()
        cond[...] = ptab[assign_ref[0]]

    def front(i, c):
        @pl.when(s == 0)
        def _():
            @pl.when(i > 0)
            def _():
                l_copy(i, c).wait_recv()
            first = jnp.dot(latin[i, rows(c), :], cin[...].astype(BF16), preferred_element_type=F32).astype(BF16)
            xbuf[i, 0, rows(c), :] = first
            xbuf[i, 1, rows(c), :] = first

        @pl.when(s > 0)
        def _():
            x_copy(ybuf.at[i, :, rows(c), :], i, c).wait_recv()

        k_copy(ybuf.at[i, :, rows(c), :], i, c).wait_recv()
        time_vec = tv[pl.ds(i, 1), :]
        for g in range(2):
            a = 0.5 * (xbuf[i, g, rows(c), :].astype(F32) + kbuf[i, g, rows(c), :].astype(F32)) + time_vec
            if g == 0:
                a = a + cond[...]
            a_scr[c, g * part:(g + 1) * part, :] = a
        a = a_scr[c]
        normed = (a * lax.rsqrt(jnp.mean(a * a, axis=-1, keepdims=True) + 1e-6)).astype(BF16)
        tile = 256 if hidden % 256 == 0 else hidden
        for j in range(0, hidden, tile):
            gate = jnp.dot(normed, w_in[:, hidden + j:hidden + j + tile], preferred_element_type=F32)
            value = jnp.dot(normed, w_in[:, j:j + tile], preferred_element_type=F32)
            gelu = 0.5 * gate * (1.0 + lax.erf(gate * math.sqrt(0.5)))
            h_scr[c, :, j:j + tile] = (value * gelu).astype(BF16)

    def back(i, c):
        out = (a_scr[c] + jnp.dot(h_scr[c], w_all[...], preferred_element_type=F32)).astype(BF16)

        @pl.when(i < steps - 1)
        def _():
            ybuf[i + 1, :, rows(c), :] = out.reshape(2, part, channels)

            @pl.when(s < last)
            def _():
                x_copy(ybuf.at[i + 1, :, rows(c), :], i + 1, c).start()
            k_copy(ybuf.at[i + 1, :, rows(c), :], i + 1, c).start()

        @pl.when(i == steps - 1)
        def _():
            oseg_ref[:, rows(c), :] = out.reshape(2, part, channels)

        @pl.when(s == last)
        def _():
            v = out.astype(F32)
            v = v * lax.rsqrt(jnp.mean(v * v, axis=-1, keepdims=True) + 1e-6)
            m = (v * (1.0 / (1.0 + jnp.exp(-v)))).astype(BF16)
            e = lax.dot_general(m, cout[...].astype(BF16), (((1,), (1,)), ((), ())), preferred_element_type=F32)
            guided = e[part:] + guidance_scale * (e[:part] - e[part:])
            root_now, root_next = roots[pl.ds(i, 1), :], roots[pl.ds(i + 1, 1), :]
            rest_now, rest_next = rests[pl.ds(i, 1), :], rests[pl.ds(i + 1, 1), :]
            clean = (lat[rows(c), :] - rest_now * guided) / root_now
            new = root_next * clean + rest_next * guided
            lat[rows(c), :] = new

            @pl.when(i < steps - 1)
            def _():
                latout[i + 1, rows(c), :] = new.astype(BF16)
                l_copy(i + 1, c).start()

    def pass_on(k):
        @pl.when(z >= k)
        def _():
            b = me - 2 * k
            g_arrived(b)

            @pl.when(z < length - 1)
            def _():
                g_copy(b, me + 2, g_line.at[0]).start()
            g_copy(b, side, g_side).start()

        @pl.when(z + k < length)
        def _():
            b = me + 2 * k
            g_arrived(b)

            @pl.when(z > 0)
            def _():
                g_copy(b, me - 2, g_line.at[1]).start()
            g_copy(b, side, g_side).start()

    if not gathered:
        pass_on(1)
    loads[1].wait()
    for c in range(CHUNKS):
        front(0, c)
    loads[2].wait()
    if not gathered:
        for k in range(2, length):
            pass_on(k)
        for k in range(length):
            g_arrived(2 * k + (1 - y))
    for c in range(CHUNKS):
        back(0, c)

    def body(i, carry):
        for c in range(CHUNKS):
            front(i, c)
            back(i, c)
        return carry

    lax.fori_loop(1, steps, body, 0)

    @pl.when(s == last)
    def _():
        turned = lat[...].T
        here = olat_ref.shape[0]
        for d in range(sects):
            fin[d] = turned[d * here:(d + 1) * here, :]
        for d in range(sects - 1):
            f_copy(d).start()
        olat_ref[...] = fin[last]
        for d in range(sects - 1):
            f_copy(d).wait_send()
        for i in range(1, steps):
            for c in range(CHUNKS):
                l_copy(i, c).wait_send()

    @pl.when(s < last)
    def _():
        f_copy(0).wait_recv()
        olat_ref[...] = fin_in[...]
        for i in range(steps):
            for c in range(CHUNKS):
                x_copy(ybuf.at[i, :, rows(c), :], i, c).wait_send()

    for i in range(steps):
        for c in range(CHUNKS):
            k_copy(ybuf.at[i, :, rows(c), :], i, c).wait_send()
    if not gathered:
        for d in range(1, batches):
            p_copy(d).wait_send()
        for k in range(length):
            @pl.when(z >= k)
            def _(k=k):
                b = me - 2 * k

                @pl.when(z < length - 1)
                def _():
                    g_copy(b, me + 2, g_line.at[0]).wait_send()
                g_copy(b, side, g_side).wait_send()

            @pl.when(z + k < length)
            def _(k=k):
                b = me + 2 * k

                @pl.when(z > 0)
                def _():
                    g_copy(b, me - 2, g_line.at[1]).wait_send()
                if k > 0:
                    g_copy(b, side, g_side).wait_send()


def on_device(
    sects, batches, warm, latents, timesteps, assign, prompts, w_in, time_w, w_out, conv_in_w, conv_out_w
):
    positions = latents.shape[1]
    channels = warm.shape[1]
    hidden = w_out.shape[0] * batches
    steps = timesteps.shape[0] - 1
    gathered = w_out.shape[0] % 16 != 0 or batches % 2 != 0
    if gathered:
        w_out = lax.all_gather(w_out, "batch", axis=0, tiled=True)
        table = lax.all_gather(prompts, "batch", axis=0, tiled=True)
        prompts = lax.dynamic_slice_in_dim(table, assign[0], 1, 0).astype(F32)
    whole = pl.BlockSpec(memory_space=pltpu.VMEM)
    apart = pl.BlockSpec(memory_space=pl.ANY)
    scalars = pl.BlockSpec(memory_space=pltpu.SMEM)
    here = latents.shape[0] // sects
    dma = pltpu.SemaphoreType.DMA
    width = 2 * positions // CHUNKS
    segment, final = pl.pallas_call(
        functools.partial(kernel, sects, batches, gathered),
        out_shape=(
            jax.ShapeDtypeStruct((2, positions, channels), BF16),
            jax.ShapeDtypeStruct((here, positions), F32),
        ),
        in_specs=[scalars, scalars, apart, whole, whole, apart, apart, apart, whole, whole],
        out_specs=(whole, whole),
        scratch_shapes=[
            pltpu.VMEM(w_in.shape, BF16),
            pltpu.VMEM(time_w.shape, BF16),
            pltpu.VMEM((hidden, channels), BF16),
            pltpu.VMEM((steps, 2, positions, channels), BF16),
            pltpu.VMEM((steps, 2, positions, channels), BF16),
            pltpu.VMEM((steps, 2, positions, channels), BF16),
            pltpu.VMEM((CHUNKS, width, channels), F32),
            pltpu.VMEM((CHUNKS, width, hidden), BF16),
            pltpu.VMEM((16, channels), F32),
            pltpu.VMEM((16, 128), F32),
            pltpu.VMEM((16, 128), F32),
            pltpu.VMEM((1, channels), F32),
            pltpu.VMEM((batches, 1, channels), F32),
            pltpu.VMEM((1, channels), F32),
            pltpu.VMEM((128, channels), F32),
            pltpu.VMEM((128, channels), F32),
            pltpu.VMEM((128, positions), F32),
            pltpu.VMEM((steps, positions, 128), BF16),
            pltpu.VMEM((steps, positions, 128), BF16),
            pltpu.VMEM((sects, here, positions), F32),
            pltpu.VMEM((here, positions), F32),
            dma((3,)),
            dma((steps, CHUNKS)), dma((steps, CHUNKS)),
            dma((steps, CHUNKS)), dma((steps, CHUNKS)),
            dma((steps, CHUNKS)), dma((steps, CHUNKS)),
            dma((sects,)), dma(()),
            dma((batches,)), dma((batches,)),
            dma((2, batches)), dma((batches,)), dma((batches,)),
        ],
        compiler_params=pltpu.CompilerParams(
            collective_id=0, has_side_effects=True, vmem_limit_bytes=40 * 1024 * 1024
        ),
    )(
        timesteps, assign, warm.reshape(2, positions, channels), latents, prompts,
        w_in, time_w, w_out, conv_in_w, conv_out_w,
    )
    return segment.reshape(2 * positions, channels), final


def solution(mesh):
    return jax.shard_map(
        functools.partial(on_device, mesh.shape["sect"], mesh.shape["batch"]),
        mesh=mesh,
        in_specs=(
            P(("sect", "batch"), None),
            P(None, "batch"),
            P(),
            P("batch"),
            P("batch", None),
            P("sect", None),
            P("sect", None),
            P(("sect", "batch"), None),
            P(),
            P(),
        ),
        out_specs=(P(("sect", "batch"), None), P("sect", "batch")),
        check_vma=False,
    )
```

time: 148 us -> 65.5 us (0.44)
  blocking collectives: 66.5 us -> 0 us
  Pallas kernels: 0 us -> 54.2 us
  matrix products: 41 us -> 0 us
  between operations: 19.2 us -> 1.3 us
  starting transfers between devices: 11.1 us -> 0 us
  local copies, waits for them, and re-layouts: 2.51 us -> 9.6 us
  other arithmetic: 6.24 us -> 0 us
    pallas_call x0 -> x1, Pallas kernels: none -> 54.2 us  [on_device(): pl.pallas_call(functools.partial(kernel, sects, batches, gathered), out_s...]
    dot_general x21 -> x0, matrix products: 41 us -> none  [the longest x4 21.4 us: feed_block(): jnp.dot(hidden, weight_out, preferred_element_type=jnp.float32)]
    psum x4 -> x0, blocking collectives: 35.2 us -> none  [broadcast(): return lax.psum(block, axis)]
    all_gather x1 -> x0, blocking collectives: 31.3 us -> none  [on_device(): lax.all_gather(prompts, 'batch', axis=0, tiled=True)]
    ppermute x8 -> x0, starting transfers between devices: 11 us -> none  [the longest x4 10.2 us: passed_along(): return lax.ppermute(shard, axis, pairs)]
    unnamed x26 -> x20, local copies, waits for them, and re-layouts: 0.43 us -> 9.6 us
    reduce_sum x4 -> x0, other arithmetic: 5.44 us -> none  [rms_norm(): jnp.mean(values * values, axis=-1, keepdims=True) + 1e-06]
    slice x1 -> x0, local copies, waits for them, and re-layouts: 1.51 us -> none  [on_device(): time_next = timesteps[step_index + 1]]
  transfers between devices with their start and end apart: 9 -> 0, of which waited for: 0 -> 0; matrix products, arithmetic and copies ran while one was open for 11% -> 0% of each run, Pallas kernels for 0% -> 0%
where the time goes in v1:
time: 65.5 us; the launch traced here: 65.1 us
  Pallas kernels  54.2 us (83%)
  local copies, waits for them, and re-layouts  9.6 us (15%)
  between operations  1.3 us (2%)
    pallas_call x1, Pallas kernels, on_device(): pl.pallas_call(functools.partial(kernel, sects, batches, gathered), out_s...  54.2 us
    unnamed x20, local copies, waits for them, and re-layouts  9.6 us

profile of v1, /device:TPU:0, one launch (start us, length us, event | category | flops | bytes accessed | tf_op | source)
XLA Modules:
  0.0 65.1 jit_solution(2670550569871525997)
XLA Ops:
  1.3 0.0 copy-start
  1.3 1.9 %copy-done = bf16[640,2560]{1,0:T(8,128)(2,1)S(1)} copy-done((bf16[640,2560]{1,0:T(8,128)(2,1)S(1)}, bf16[640,2560]{1,0:T(8,128)(2,1)}, u32[]{:S(2)}) %copy-start) | copy-done | bytes 3276824
  3.2 0.0 copy-start.1
  3.2 1.1 %copy-done.1 = bf16[640,640]{1,0:T(8,128)(2,1)S(1)} copy-done((bf16[640,640]{1,0:T(8,128)(2,1)S(1)}, bf16[640,640]{1,0:T(8,128)(2,1)}, u32[]{:S(2)}) %copy-start.1) | copy-done | bytes 819224
  4.4 0.0 copy-start.2
  4.4 1.0 %copy-done.2 = bf16[256,640]{1,0:T(8,128)(2,1)S(1)} copy-done((bf16[256,640]{1,0:T(8,128)(2,1)S(1)}, bf16[256,640]{1,0:T(8,128)(2,1)}, u32[]{:S(2)}) %copy-start.2) | copy-done | bytes 327704
  5.3 0.0 copy-start.3
  5.3 0.9 %copy-done.3 = bf16[160,640]{1,0:T(8,128)(2,1)S(1)} copy-done((bf16[160,640]{1,0:T(8,128)(2,1)S(1)}, bf16[160,640]{1,0:T(8,128)(2,1)}, u32[]{:S(2)}) %copy-start.3) | copy-done | bytes 204824
  6.3 0.0 copy-start.4
  6.3 0.7 %copy-done.4 = bf16[4,640]{1,0:T(4,128)(2,1)S(1)} copy-done((bf16[4,640]{1,0:T(4,128)(2,1)S(1)}, bf16[4,640]{1,0:T(4,128)(2,1)}, u32[]{:S(2)}) %copy-start.4) | copy-done | bytes 5144
  6.9 0.0 copy-start.5
  6.9 0.7 %copy-done.5 = bf16[4,640]{1,0:T(4,128)(2,1)S(1)} copy-done((bf16[4,640]{1,0:T(4,128)(2,1)S(1)}, bf16[4,640]{1,0:T(4,128)(2,1)}, u32[]{:S(2)}) %copy-start.5) | copy-done | bytes 5144
  7.6 0.0 copy-start.6
  7.6 0.7 %copy-done.6 = bf16[1,640]{1,0:T(2,128)(2,1)S(1)} copy-done((bf16[1,640]{1,0:T(2,128)(2,1)S(1)}, bf16[1,640]{1,0:T(2,128)(2,1)}, u32[]{:S(2)}) %copy-start.6) | copy-done | bytes 1304
  8.3 0.0 copy-start.7
  8.3 0.7 %copy-done.7 = f32[4,128]{1,0:T(4,128)S(1)} copy-done((f32[4,128]{1,0:T(4,128)S(1)}, f32[4,128]{1,0:T(4,128)}, u32[]{:S(2)}) %copy-start.7) | copy-done | bytes 2072
  9.0 0.0 copy-start.8
  9.0 0.7 %copy-done.8 = s32[5]{0:T(128)S(1)} copy-done((s32[5]{0:T(128)S(1)}, s32[5]{0:T(128)}, u32[]{:S(2)}) %copy-start.8) | copy-done | bytes 44
  9.7 54.2 %shard_map.113 = (bf16[2,128,640]{2,1,0:T(8,128)(2,1)S(1)}, f32[1,128]{1,0:T(1,128)S(1)}) custom-call(s32[5]{0:T(128)S(1)} %copy-done.8, s32[1]{0:T(128)S(6)} %copy.14.assign_ref, bf16[2,128,640]{2,1,0:T(8,128)(2,1)S(1)} %bitcast.2, f32[4,128]{1,0:T(4,128)S(1)} %copy-done.7, bf16[1,640]{1,0:T(2,128)(2,1)S(1)} %copy-done.6, bf16[640,2560]{1,0:T(8,128)(2,1)S(1)} %copy-done, ...), custom_call_target="tpu_custom_call" | custom-call | tf_op jit(solution)/shard_map/pallas_call | solution.py:335
  63.8 0.7 %copy.15 = bf16[256,640]{1,0:T(8,128)(2,1)} copy(bf16[256,640]{1,0:T(8,128)(2,1)S(1)} %bitcast.3) | data formatting | bytes 655360
  64.5 0.5 copy.16
Async XLA Ops:
  1.3 1.9 %copy-start = (bf16[640,2560]{1,0:T(8,128)(2,1)S(1)}, bf16[640,2560]{1,0:T(8,128)(2,1)}, u32[]{:S(2)}) copy-start(bf16[640,2560]{1,0:T(8,128)(2,1)} %w_in_ref.1) | copy-start | bytes 9830404
  3.2 1.1 %copy-start.1 = (bf16[640,640]{1,0:T(8,128)(2,1)S(1)}, bf16[640,640]{1,0:T(8,128)(2,1)}, u32[]{:S(2)}) copy-start(bf16[640,640]{1,0:T(8,128)(2,1)} %time_w_ref.1) | copy-start | bytes 2457604
  4.4 1.0 %copy-start.2 = (bf16[256,640]{1,0:T(8,128)(2,1)S(1)}, bf16[256,640]{1,0:T(8,128)(2,1)}, u32[]{:S(2)}) copy-start(bf16[256,640]{1,0:T(8,128)(2,1)} %param.10) | copy-start | bytes 983044
  5.3 0.9 %copy-start.3 = (bf16[160,640]{1,0:T(8,128)(2,1)S(1)}, bf16[160,640]{1,0:T(8,128)(2,1)}, u32[]{:S(2)}) copy-start(bf16[160,640]{1,0:T(8,128)(2,1)} %w_out_ref.1) | copy-start | bytes 614404
  6.3 0.7 %copy-start.4 = (bf16[4,640]{1,0:T(4,128)(2,1)S(1)}, bf16[4,640]{1,0:T(4,128)(2,1)}, u32[]{:S(2)}) copy-start(bf16[4,640]{1,0:T(4,128)(2,1)} %cin_ref.1) | copy-start | bytes 15364
  6.9 0.7 %copy-start.5 = (bf16[4,640]{1,0:T(4,128)(2,1)S(1)}, bf16[4,640]{1,0:T(4,128)(2,1)}, u32[]{:S(2)}) copy-start(bf16[4,640]{1,0:T(4,128)(2,1)} %cout_ref.1) | copy-start | bytes 15364
  7.6 0.7 %copy-start.6 = (bf16[1,640]{1,0:T(2,128)(2,1)S(1)}, bf16[1,640]{1,0:T(2,128)(2,1)}, u32[]{:S(2)}) copy-start(bf16[1,640]{1,0:T(2,128)(2,1)} %prompts_ref.1) | copy-start | bytes 3844
  8.3 0.7 %copy-start.7 = (f32[4,128]{1,0:T(4,128)S(1)}, f32[4,128]{1,0:T(4,128)}, u32[]{:S(2)}) copy-start(f32[4,128]{1,0:T(4,128)} %lat_ref.1) | copy-start | bytes 6148
  9.0 0.7 %copy-start.8 = (s32[5]{0:T(128)S(1)}, s32[5]{0:T(128)}, u32[]{:S(2)}) copy-start(s32[5]{0:T(128)} %ts_ref.1) | copy-start | bytes 64

commit v2 on v1

--- a/solution.py
+++ b/solution.py
@@ -17,8 +17,9 @@
 
 def kernel(
     sects, batches, gathered,
-    ts_ref, assign_ref, warm_ref, lat_ref, prompts_ref, w_in_ref, time_w_ref, w_out_ref, cin_ref, cout_ref,
+    ts_hbm, assign_hbm, warm_ref, lat_hbm, prompts_hbm, w_in_ref, time_w_ref, w_out_ref, cin_hbm, cout_hbm,
     oseg_ref, olat_ref,
+    ts_ref, assign_ref, lat_ref, prompts_ref, cin_ref, cout_ref,
     w_in, time_w, w_all, xbuf, kbuf, ybuf, a_scr, h_scr, tv, roots, rests, cond, ptab, pown,
     cin, cout, lat, latin, latout, fin, fin_in,
     load_sem, x_send, x_recv, k_send, k_recv, l_send, l_recv, f_send, f_recv,
@@ -44,7 +45,11 @@
         depth = w_out_ref.shape[0]
         own_rows = pl.ds(pl.multiple_of(me * depth, depth), depth)
         loads.append(pltpu.make_async_copy(w_out_ref, w_all.at[own_rows], load_sem.at[2]))
-    for copy in loads:
+    pairs = [(prompts_hbm, prompts_ref), (ts_hbm, ts_ref), (assign_hbm, assign_ref), (lat_hbm, lat_ref),
+             (cin_hbm, cin_ref), (cout_hbm, cout_ref)]
+    for j, (src, dst) in enumerate(pairs):
+        loads.append(pltpu.make_async_copy(src, dst, load_sem.at[3 + j]))
+    for copy in loads[3:] + loads[:3]:
         copy.start()
 
     barrier = pltpu.get_barrier_semaphore()
@@ -55,6 +60,7 @@
         for d in range(1, batches):
             pl.semaphore_signal(barrier, inc=1, device_id={"batch": lax.rem(me + d, batches)}, device_id_type=MESH)
         met += batches - 1
+        loads[3].wait()
         pown[...] = prompts_ref[...].astype(F32)
     pl.semaphore_wait(barrier, met)
 
@@ -121,6 +127,10 @@
             x_copy(warm_ref.at[:, rows(c), :], 0, c).start()
         k_copy(warm_ref.at[:, rows(c), :], 0, c).start()
 
+    if gathered:
+        loads[3].wait()
+    for copy in loads[4:]:
+        copy.wait()
     cin[...] = jnp.zeros_like(cin)
     cout[...] = jnp.zeros_like(cout)
     levels = cin_ref.shape[0]
@@ -327,8 +337,7 @@
         table = lax.all_gather(prompts, "batch", axis=0, tiled=True)
         prompts = lax.dynamic_slice_in_dim(table, assign[0], 1, 0).astype(F32)
     whole = pl.BlockSpec(memory_space=pltpu.VMEM)
-    apart = pl.BlockSpec(memory_space=pl.ANY)
-    scalars = pl.BlockSpec(memory_space=pltpu.SMEM)
+    apart = pl.BlockSpec(memory_space=pltpu.HBM)
     here = latents.shape[0] // sects
     dma = pltpu.SemaphoreType.DMA
     width = 2 * positions // CHUNKS
@@ -338,9 +347,15 @@
             jax.ShapeDtypeStruct((2, positions, channels), BF16),
             jax.ShapeDtypeStruct((here, positions), F32),
         ),
-        in_specs=[scalars, scalars, apart, whole, whole, apart, apart, apart, whole, whole],
+        in_specs=[apart] * 10,
         out_specs=(whole, whole),
         scratch_shapes=[
+            pltpu.SMEM(timesteps.shape, jnp.int32),
+            pltpu.SMEM(assign.shape, jnp.int32),
+            pltpu.VMEM(latents.shape, F32),
+            pltpu.VMEM(prompts.shape, prompts.dtype),
+            pltpu.VMEM(conv_in_w.shape, BF16),
+            pltpu.VMEM(conv_out_w.shape, BF16),
             pltpu.VMEM(w_in.shape, BF16),
             pltpu.VMEM(time_w.shape, BF16),
             pltpu.VMEM((hidden, channels), BF16),
@@ -362,7 +377,7 @@
             pltpu.VMEM((steps, positions, 128), BF16),
             pltpu.VMEM((sects, here, positions), F32),
             pltpu.VMEM((here, positions), F32),
-            dma((3,)),
+            dma((9,)),
             dma((steps, CHUNKS)), dma((steps, CHUNKS)),
             dma((steps, CHUNKS)), dma((steps, CHUNKS)),
             dma((steps, CHUNKS)), dma((steps, CHUNKS)),
@@ -371,7 +386,7 @@
             dma((2, batches)), dma((batches,)), dma((batches,)),
         ],
         compiler_params=pltpu.CompilerParams(
-            collective_id=0, has_side_effects=True, vmem_limit_bytes=40 * 1024 * 1024
+            collective_id=0, has_side_effects=True, vmem_limit_bytes=60 * 1024 * 1024
         ),
     )(
         timesteps, assign, warm.reshape(2, positions, channels), latents, prompts,

time: 65.5 us -> 58.1 us (0.89)
  local copies, waits for them, and re-layouts: 9.6 us -> 2.84 us
    unnamed x20 -> x2, local copies, waits for them, and re-layouts: 9.6 us -> 2.84 us
where the time goes in v2:
time: 58.1 us; the launch traced here: 58 us
  Pallas kernels  53.8 us (93%)
  local copies, waits for them, and re-layouts  2.84 us (5%)
  between operations  1.29 us (2%)
    pallas_call x1, Pallas kernels, on_device(): pl.pallas_call(functools.partial(kernel, sects, batches, gathered), out_s...  53.8 us
    unnamed x2, local copies, waits for them, and re-layouts  2.84 us

profile of v2, /device:TPU:0, one launch (start us, length us, event | category | flops | bytes accessed | tf_op | source)
XLA Modules:
  0.0 58.0 jit_solution(2059327012110206238)
XLA Ops:
  1.3 53.8 %shard_map.113 = (bf16[2,128,640]{2,1,0:T(8,128)(2,1)}, f32[1,128]{1,0:T(1,128)}) custom-call(s32[5]{0:T(128)} %ts_hbm.1, s32[1]{0:T(128)S(6)} %copy.14.assign_hbm, bf16[2,128,640]{2,1,0:T(8,128)(2,1)} %bitcast.2, f32[4,128]{1,0:T(4,128)} %lat_hbm.1, bf16[1,640]{1,0:T(2,128)(2,1)} %prompts_hbm.1, bf16[640,2560]{1,0:T(8,128)(2,1)} %w_in_ref.1, ...), custom_call_target="tpu_custom_call" | custom-call | tf_op jit(solution)/shard_map/pallas_call | solution.py:344
  55.1 1.7 %copy.15 = bf16[256,640]{1,0:T(8,128)(2,1)} copy(bf16[256,640]{1,0:T(8,128)(2,1)} %bitcast.3) | data formatting | bytes 655360
  56.9 1.1 %copy.16 = f32[1,128]{1,0:T(1,128)} copy(f32[1,128]{1,0:T(1,128)} %get-tuple-element.9) | data formatting | bytes 1024

commit v3 on v2

--- a/solution.py
+++ b/solution.py
@@ -13,6 +13,12 @@
 F32 = jnp.float32
 BF16 = jnp.bfloat16
 CHUNKS = 2
+SPLIT = (384, 256)
+
+
+def column_pieces(channels):
+    widths = SPLIT if sum(SPLIT) == channels else (channels,)
+    return [(sum(widths[:j]), width) for j, width in enumerate(widths)]
 
 
 def kernel(
@@ -23,7 +29,7 @@
     w_in, time_w, w_all, xbuf, kbuf, ybuf, a_scr, h_scr, tv, roots, rests, cond, ptab, pown,
     cin, cout, lat, latin, latout, fin, fin_in,
     load_sem, x_send, x_recv, k_send, k_recv, l_send, l_recv, f_send, f_recv,
-    p_send, p_recv, g_line, g_side, g_recv,
+    p_send, p_recv, g_line, g_side, g_recv, xc_send, xc_recv, kc_send, kc_recv,
 ):
     s = lax.axis_index("sect")
     me = lax.axis_index("batch")
@@ -34,6 +40,8 @@
     up = lax.rem(s + 1, sects)
     down = lax.rem(s + sects - 1, sects)
     last = sects - 1
+    pieces = column_pieces(channels)
+    final_piece = len(pieces) - 1
 
     loads = [
         pltpu.make_async_copy(time_w_ref, time_w, load_sem.at[0]),
@@ -77,6 +85,22 @@
             src_ref=src, dst_ref=kbuf.at[slot, :, rows(c), :], send_sem=k_send.at[slot, c],
             recv_sem=k_recv.at[slot, c], device_id={"sect": down}, device_id_type=MESH)
 
+    def columns(ref, j, c=None):
+        at, width = pieces[j]
+        return ref.at[1, :, slice(None) if c is None else rows(c), pl.ds(at, width)]
+
+    def x_part(j, c=None):
+        sems = (xc_send.at[j], xc_recv.at[j]) if c is None else (x_send.at[1, c], x_recv.at[1, c])
+        return pltpu.make_async_remote_copy(
+            src_ref=columns(ybuf, j, c), dst_ref=columns(xbuf, j, c), send_sem=sems[0],
+            recv_sem=sems[1], device_id={"sect": up}, device_id_type=MESH)
+
+    def k_part(j, c=None):
+        sems = (kc_send.at[j], kc_recv.at[j]) if c is None else (k_send.at[1, c], k_recv.at[1, c])
+        return pltpu.make_async_remote_copy(
+            src_ref=columns(ybuf, j, c), dst_ref=columns(kbuf, j, c), send_sem=sems[0],
+            recv_sem=sems[1], device_id={"sect": down}, device_id_type=MESH)
+
     def l_copy(slot, c):
         return pltpu.make_async_remote_copy(
             src_ref=latout.at[slot, rows(c), :], dst_ref=latin.at[slot, rows(c), :], send_sem=l_send.at[slot, c],
@@ -97,29 +121,102 @@
                 src_ref=pown, dst_ref=ptab.at[me], send_sem=p_send.at[d], recv_sem=p_recv.at[me],
                 device_id={"batch": lax.rem(me + d, batches)}, device_id_type=MESH)
 
-        def block(b):
-            return w_all.at[pl.ds(pl.multiple_of(b * depth, depth), depth)]
-
-        def g_copy(b, to, sems, src=None):
+        def block(j, b):
+            at, width = pieces[j]
+            return w_all.at[pl.ds(pl.multiple_of(b * depth, depth), depth), pl.ds(at, width)]
+
+        def g_copy(j, b, to, sem, own=False):
+            at, width = pieces[j]
             return pltpu.make_async_remote_copy(
-                src_ref=block(b) if src is None else src, dst_ref=block(b), send_sem=sems.at[b],
-                recv_sem=g_recv.at[b], device_id={"batch": to}, device_id_type=MESH)
-
-        def g_arrived(b):
-            pltpu.make_async_copy(block(b), block(b), g_recv.at[b]).wait()
+                src_ref=w_out_ref.at[:, pl.ds(at, width)] if own else block(j, b), dst_ref=block(j, b), send_sem=sem,
+                recv_sem=g_recv.at[j, b], device_id={"batch": to}, device_id_type=MESH)
+
+        def g_up(j, b, own=False):
+            return g_copy(j, b, me + 2, g_line.at[0, j, b], own)
+
+        def g_down(j, b, own=False):
+            return g_copy(j, b, me - 2, g_line.at[1, j, b], own)
+
+        def g_side_copy(j, b, own=False):
+            return g_copy(j, b, side, g_side.at[j, b], own)
+
+        def g_arrived(j, b):
+            pltpu.make_async_copy(block(j, b), block(j, b), g_recv.at[j, b]).wait()
+
+        middle = 1 if len(pieces) > 1 else -1
+
+        def own(j, act):
+            @pl.when(z < length - 1)
+            def _():
+                act(g_up(j, me, True))
+
+            @pl.when(z > 0)
+            def _():
+                act(g_down(j, me, True))
+            act(g_side_copy(j, me, True))
+
+        def pass_on(j, k, act, arrive):
+            @pl.when(z >= k)
+            def _():
+                b = me - 2 * k
+                if arrive:
+                    g_arrived(j, b)
+
+                @pl.when(z < length - 1)
+                def _():
+                    act(g_up(j, b))
+                if not (j == middle and k == 1):
+                    act(g_side_copy(j, b))
+
+            @pl.when(z + k < length)
+            def _():
+                b = me + 2 * k
+                if arrive:
+                    g_arrived(j, b)
+
+                @pl.when(z > 0)
+                def _():
+                    act(g_down(j, b))
+                if j == middle and k == 1:
+                    @pl.when(z > 0)
+                    def _():
+                        act(g_side_copy(j, b))
+                else:
+                    act(g_side_copy(j, b))
+
+        def extra(act, arrive):
+            if arrive:
+                g_arrived(middle, side)
+
+            @pl.when(z < length - 1)
+            def _():
+                act(g_up(middle, side))
+
+            @pl.when(z == 1)
+            def _():
+                act(g_down(middle, side))
+
+        def start(copy):
+            copy.start()
+
+        def sent(copy):
+            copy.wait_send()
+
+        def piece_here(j):
+            for k in range(length):
+                b = 2 * k + (1 - y)
+                if j == middle:
+                    @pl.when(b != side)
+                    def _():
+                        g_arrived(j, b)
+                else:
+                    g_arrived(j, b)
 
         for d in range(1, batches):
             p_copy(d).start()
-
-        @pl.when(z < length - 1)
-        def _():
-            g_copy(me, me + 2, g_line.at[0], w_out_ref).start()
-
-        @pl.when(z > 0)
-        def _():
-            g_copy(me, me - 2, g_line.at[1], w_out_ref).start()
-
-        g_copy(me, side, g_side, w_out_ref).start()
+        own(0, start)
+        if final_piece > 0:
+            own(1, start)
 
     for c in range(CHUNKS):
         @pl.when(s < last)
@@ -167,7 +264,7 @@
             pltpu.make_async_copy(ptab.at[b], ptab.at[b], p_recv.at[b]).wait()
         cond[...] = ptab[assign_ref[0]]
 
-    def front(i, c):
+    def front(i, c, parts=False):
         @pl.when(s == 0)
         def _():
             @pl.when(i > 0)
@@ -179,9 +276,21 @@
 
         @pl.when(s > 0)
         def _():
-            x_copy(ybuf.at[i, :, rows(c), :], i, c).wait_recv()
-
-        k_copy(ybuf.at[i, :, rows(c), :], i, c).wait_recv()
+            if parts:
+                if c == 0:
+                    for j in range(final_piece):
+                        x_part(j).wait_recv()
+                x_part(final_piece, c).wait_recv()
+            else:
+                x_copy(ybuf.at[i, :, rows(c), :], i, c).wait_recv()
+
+        if parts:
+            if c == 0:
+                for j in range(final_piece):
+                    k_part(j).wait_recv()
+            k_part(final_piece, c).wait_recv()
+        else:
+            k_copy(ybuf.at[i, :, rows(c), :], i, c).wait_recv()
         time_vec = tv[pl.ds(i, 1), :]
         for g in range(2):
             a = 0.5 * (xbuf[i, g, rows(c), :].astype(F32) + kbuf[i, g, rows(c), :].astype(F32)) + time_vec
@@ -212,7 +321,20 @@
         @pl.when(i == steps - 1)
         def _():
             oseg_ref[:, rows(c), :] = out.reshape(2, part, channels)
-
+        denoise(i, c, out)
+
+    def back_piece(j, c):
+        at, width = pieces[j]
+        out = a_scr[c, :, at:at + width] + jnp.dot(h_scr[c], w_all[:, at:at + width], preferred_element_type=F32)
+        ybuf[1, :, rows(c), at:at + width] = out.astype(BF16).reshape(2, part, width)
+
+    def send_piece(j, c=None):
+        @pl.when(s < last)
+        def _():
+            x_part(j, c).start()
+        k_part(j, c).start()
+
+    def denoise(i, c, out):
         @pl.when(s == last)
         def _():
             v = out.astype(F32)
@@ -231,40 +353,49 @@
                 latout[i + 1, rows(c), :] = new.astype(BF16)
                 l_copy(i + 1, c).start()
 
-    def pass_on(k):
-        @pl.when(z >= k)
-        def _():
-            b = me - 2 * k
-            g_arrived(b)
-
-            @pl.when(z < length - 1)
-            def _():
-                g_copy(b, me + 2, g_line.at[0]).start()
-            g_copy(b, side, g_side).start()
-
-        @pl.when(z + k < length)
-        def _():
-            b = me + 2 * k
-            g_arrived(b)
-
-            @pl.when(z > 0)
-            def _():
-                g_copy(b, me - 2, g_line.at[1]).start()
-            g_copy(b, side, g_side).start()
-
-    if not gathered:
-        pass_on(1)
-    loads[1].wait()
+    def back_pieces(j):
+        for c in range(CHUNKS):
+            back_piece(j, c)
+            if j == final_piece:
+                send_piece(j, c)
+                denoise(0, c, ybuf[1, :, rows(c), :].reshape(2 * part, channels))
+        if j < final_piece:
+            send_piece(j)
+
+    def fronts(c):
+        if c == 0:
+            loads[1].wait()
+        front(0, c)
+
+    if gathered:
+        for c in range(CHUNKS):
+            fronts(c)
+        loads[2].wait()
+        for j in range(len(pieces)):
+            back_pieces(j)
+    else:
+        for k in range(1, length):
+            pass_on(0, k, start, True)
+        if middle == 1:
+            extra(start, True)
+            pass_on(1, 1, start, True)
+        fronts(0)
+        for j in range(2, len(pieces)):
+            own(j, start)
+        if middle == 1 and length > 2:
+            pass_on(1, 2, start, True)
+        for c in range(1, CHUNKS):
+            fronts(c)
+        loads[2].wait()
+        for j in range(len(pieces)):
+            if j + 1 < len(pieces):
+                for k in range(3 if j == 0 else 1, length):
+                    pass_on(j + 1, k, start, True)
+            piece_here(j)
+            back_pieces(j)
     for c in range(CHUNKS):
-        front(0, c)
-    loads[2].wait()
-    if not gathered:
-        for k in range(2, length):
-            pass_on(k)
-        for k in range(length):
-            g_arrived(2 * k + (1 - y))
-    for c in range(CHUNKS):
-        back(0, c)
+        front(1, c, True)
+        back(1, c)
 
     def body(i, carry):
         for c in range(CHUNKS):
@@ -272,7 +403,7 @@
             back(i, c)
         return carry
 
-    lax.fori_loop(1, steps, body, 0)
+    lax.fori_loop(2, steps, body, 0)
 
     @pl.when(s == last)
     def _():
@@ -293,35 +424,32 @@
     def _():
         f_copy(0).wait_recv()
         olat_ref[...] = fin_in[...]
+        for c in range(CHUNKS):
+            for i in range(steps):
+                if i == 1:
+                    x_part(final_piece, c).wait_send()
+                else:
+                    x_copy(ybuf.at[i, :, rows(c), :], i, c).wait_send()
+        for j in range(final_piece):
+            x_part(j).wait_send()
+
+    for c in range(CHUNKS):
         for i in range(steps):
-            for c in range(CHUNKS):
-                x_copy(ybuf.at[i, :, rows(c), :], i, c).wait_send()
-
-    for i in range(steps):
-        for c in range(CHUNKS):
-            k_copy(ybuf.at[i, :, rows(c), :], i, c).wait_send()
+            if i == 1:
+                k_part(final_piece, c).wait_send()
+            else:
+                k_copy(ybuf.at[i, :, rows(c), :], i, c).wait_send()
+    for j in range(final_piece):
+        k_part(j).wait_send()
     if not gathered:
         for d in range(1, batches):
             p_copy(d).wait_send()
-        for k in range(length):
-            @pl.when(z >= k)
-            def _(k=k):
-                b = me - 2 * k
-
-                @pl.when(z < length - 1)
-                def _():
-                    g_copy(b, me + 2, g_line.at[0]).wait_send()
-                g_copy(b, side, g_side).wait_send()
-
-            @pl.when(z + k < length)
-            def _(k=k):
-                b = me + 2 * k
-
-                @pl.when(z > 0)
-                def _():
-                    g_copy(b, me - 2, g_line.at[1]).wait_send()
-                if k > 0:
-                    g_copy(b, side, g_side).wait_send()
+        for j in range(len(pieces)):
+            own(j, sent)
+            for k in range(1, length):
+                pass_on(j, k, sent, False)
+        if middle == 1:
+            extra(sent, False)
 
 
 def on_device(
@@ -339,6 +467,7 @@
     whole = pl.BlockSpec(memory_space=pltpu.VMEM)
     apart = pl.BlockSpec(memory_space=pltpu.HBM)
     here = latents.shape[0] // sects
+    pieces = len(column_pieces(channels))
     dma = pltpu.SemaphoreType.DMA
     width = 2 * positions // CHUNKS
     segment, final = pl.pallas_call(
@@ -383,7 +512,8 @@
             dma((steps, CHUNKS)), dma((steps, CHUNKS)),
             dma((sects,)), dma(()),
             dma((batches,)), dma((batches,)),
-            dma((2, batches)), dma((batches,)), dma((batches,)),
+            dma((2, pieces, batches)), dma((pieces, batches)), dma((pieces, batches)),
+            dma((pieces,)), dma((pieces,)), dma((pieces,)), dma((pieces,)),
         ],
         compiler_params=pltpu.CompilerParams(
             collective_id=0, has_side_effects=True, vmem_limit_bytes=60 * 1024 * 1024

time: 58.1 us -> 54.8 us (0.943)
  Pallas kernels: 53.8 us -> 50.5 us
    pallas_call x1, Pallas kernels: 53.8 us -> 50.5 us  [on_device(): pl.pallas_call(functools.partial(kernel, sects, batches, gathered), out_s...]
where the time goes in v3:
time: 54.8 us; the launch traced here: 54.6 us
  Pallas kernels  50.5 us (92%)
  local copies, waits for them, and re-layouts  2.84 us (5%)
  between operations  1.29 us (2%)
    pallas_call x1, Pallas kernels, on_device(): pl.pallas_call(functools.partial(kernel, sects, batches, gathered), out_s...  50.5 us
    unnamed x2, local copies, waits for them, and re-layouts  2.84 us

profile of v3, /device:TPU:0, one launch (start us, length us, event | category | flops | bytes accessed | tf_op | source)
XLA Modules:
  0.0 54.6 jit_solution(972066603119966702)
XLA Ops:
  1.3 50.5 %shard_map.113 = (bf16[2,128,640]{2,1,0:T(8,128)(2,1)}, f32[1,128]{1,0:T(1,128)}) custom-call(s32[5]{0:T(128)} %ts_hbm.1, s32[1]{0:T(128)S(6)} %copy.14.assign_hbm, bf16[2,128,640]{2,1,0:T(8,128)(2,1)} %bitcast.2, f32[4,128]{1,0:T(4,128)} %lat_hbm.1, bf16[1,640]{1,0:T(2,128)(2,1)} %prompts_hbm.1, bf16[640,2560]{1,0:T(8,128)(2,1)} %w_in_ref.1, ...), custom_call_target="tpu_custom_call" | custom-call | tf_op jit(solution)/shard_map/pallas_call | solution.py:473
  51.7 1.7 %copy.15 = bf16[256,640]{1,0:T(8,128)(2,1)} copy(bf16[256,640]{1,0:T(8,128)(2,1)} %bitcast.3) | data formatting | bytes 655360
  53.5 1.1 %copy.16 = f32[1,128]{1,0:T(1,128)} copy(f32[1,128]{1,0:T(1,128)} %get-tuple-element.9) | data formatting | bytes 1024

commit v4 on v3

--- a/solution.py
+++ b/solution.py
@@ -13,7 +13,7 @@
 F32 = jnp.float32
 BF16 = jnp.bfloat16
 CHUNKS = 2
-SPLIT = (384, 256)
+SPLIT = (512, 128)
 
 
 def column_pieces(channels):

time: 54.8 us -> 56.1 us (1.024)
  Pallas kernels: 50.5 us -> 51.8 us
    pallas_call x1, Pallas kernels: 50.5 us -> 51.8 us  [on_device(): pl.pallas_call(functools.partial(kernel, sects, batches, gathered), out_s...]
where the time goes in v4:
time: 56.1 us; the launch traced here: 55.9 us
  Pallas kernels  51.8 us (92%)
  local copies, waits for them, and re-layouts  2.84 us (5%)
  between operations  1.29 us (2%)
    pallas_call x1, Pallas kernels, on_device(): pl.pallas_call(functools.partial(kernel, sects, batches, gathered), out_s...  51.8 us
    unnamed x2, local copies, waits for them, and re-layouts  2.84 us

profile of v4, /device:TPU:0, one launch (start us, length us, event | category | flops | bytes accessed | tf_op | source)
XLA Modules:
  0.0 55.9 jit_solution(15380613239456168126)
XLA Ops:
  1.3 51.8 %shard_map.113 = (bf16[2,128,640]{2,1,0:T(8,128)(2,1)}, f32[1,128]{1,0:T(1,128)}) custom-call(s32[5]{0:T(128)} %ts_hbm.1, s32[1]{0:T(128)S(6)} %copy.14.assign_hbm, bf16[2,128,640]{2,1,0:T(8,128)(2,1)} %bitcast.2, f32[4,128]{1,0:T(4,128)} %lat_hbm.1, bf16[1,640]{1,0:T(2,128)(2,1)} %prompts_hbm.1, bf16[640,2560]{1,0:T(8,128)(2,1)} %w_in_ref.1, ...), custom_call_target="tpu_custom_call" | custom-call | tf_op jit(solution)/shard_map/pallas_call | solution.py:473
  53.1 1.7 %copy.15 = bf16[256,640]{1,0:T(8,128)(2,1)} copy(bf16[256,640]{1,0:T(8,128)(2,1)} %bitcast.3) | data formatting | bytes 655360
  54.8 1.1 %copy.16 = f32[1,128]{1,0:T(1,128)} copy(f32[1,128]{1,0:T(1,128)} %get-tuple-element.9) | data formatting | bytes 1024
